TPU v7x, 256 devices: a whole 4x4x8 slice. The times are simulated.
256 devices in a mesh: section: 8 (over y, x_lo), dev: 32 (over x_hi, z, core).
Axes of the slice: x: 4 (x_hi: 2, x_lo: 2; x = x_hi * 2 + x_lo), y: 4, z: 8, core: 2. Of those that a mesh axis runs over, the one named last changes fastest.
Arguments:
- patches: bfloat16 [8, 49152, 1280], P('section', 'dev'), may hold values from -6 to 6
- win_count: int32 [8, 32], P('section'), may hold values from 1 to 24, 256 in all within a row
- dest_perm: int32 [8, 32], P('section'), may hold values from 0 to 31, each once within a row
- win_groups: int32 [8, 32, 24], P('section'), may hold values from 2 to 16
- norm_gain: float32 [1280], replicated, may hold values from 0.5 to 1.5
- qkv_weight: bfloat16 [1280, 3840], P('dev')
- qkv_bias: float32 [3840], replicated, may hold values from -1.5 to 1.5
- proj_weight: bfloat16 [1280, 1280], P('dev'), may hold values from -0.15625 to 0.15625
- proj_bias: float32 [1280], replicated, may hold values from -1.5 to 1.5
- merge_gain: float32 [1280], replicated, may hold values from 0.5 to 1.5
- owner: int32 [8, 4096, 1], P('section', 'dev'), may hold values from 0 to 7; in each aligned block of 128 rows (0 to 127, 128 to 255, ..., all dimensions but the last counted through in order) at most 32 rows name the same one
Outputs:
- dispatched: bfloat16 [8, 8192, 5120], P('section', 'dev')
Inputs may be any that keep to these rules, and one draw needn't show every extreme that they name: `win_count`: within each section's row the counts sum to 8 times the devices of dev, and the largest is 24. `dest_perm`: each section's row is a permutation. `win_groups`: entries of slots past a device's count are not read. Among the 128 rows of one device, at most 32 have the same owner, and some device of every draw reaches 32.
All inputs are finite; a program needn't handle non-finite values.
Results may differ from a plain program's by a relative error of at most 0.0051.
Values may be sent and summed in bfloat16 or wider, within the bound.
No kernel may reach another device: no remote copies, remote signals or barrier semaphores. Data moves between devices by JAX's collectives and lax.ppermute only.
A program may use at most 128 MiB of HBM per device.

v0:
```python
import jax
import jax.numpy as jnp
from jax import lax
from jax.sharding import PartitionSpec as P

D = 1280
HEADS = 16
WIN = 64
DST_WIN = 8
SRC_WIN = 24


def normalize(values, gain):
    return values * lax.rsqrt(jnp.mean(values * values, axis=-1, keepdims=True) + 1e-06) * gain


def contract(inputs, shard):
    whole = lax.all_gather(shard, "dev", axis=0, tiled=True)
    return jnp.dot(inputs, whole, preferred_element_type=jnp.float32)


def encode(windows, groups, norm_gain, qkv_weight, qkv_bias, proj_weight, proj_bias, merge_gain):
    count = windows.shape[0]
    values = windows.reshape(count * WIN, D).astype(jnp.float32)
    normed = normalize(values, norm_gain).astype(jnp.bfloat16)
    triple = (contract(normed, qkv_weight) + qkv_bias).astype(jnp.bfloat16)
    triple = triple.reshape(count, WIN, 3, HEADS, D // HEADS)
    scores = jnp.einsum(
        "bqhe,bkhe->bhqk", triple[:, :, 0], triple[:, :, 1], preferred_element_type=jnp.float32
    )
    scores = scores * (D // HEADS) ** (-0.5)
    living = jnp.arange(WIN, dtype=jnp.int32)[None, :] < 4 * groups[:, None]
    scores = jnp.where(living[:, None, None, :], scores, -1e30)
    highest = jnp.max(scores, axis=-1, keepdims=True)
    powers = jnp.exp(scores - highest)
    probs = (powers / jnp.sum(powers, axis=-1, keepdims=True)).astype(jnp.bfloat16)
    mixed = jnp.einsum(
        "bhqk,bkhe->bqhe", probs, triple[:, :, 2], preferred_element_type=jnp.float32
    )
    mixed = mixed.astype(jnp.bfloat16).reshape(count * WIN, D)
    encoded = values + contract(mixed, proj_weight) + proj_bias
    final = normalize(encoded, merge_gain) * living.reshape(count * WIN, 1).astype(jnp.float32)
    return final.reshape(count * WIN // 4, 4 * D).astype(jnp.bfloat16)


def pack(merged, owners, section_count, capacity):
    sections = jnp.arange(section_count, dtype=jnp.int32)
    hits = (owners[:, None] == sections[None, :]).astype(jnp.int32)
    ranks = jnp.sum((jnp.cumsum(hits, axis=0) - hits) * hits, axis=1)
    places = owners * capacity + ranks
    chosen = places[None, :] == jnp.arange(section_count * capacity, dtype=jnp.int32)[:, None]
    ladder = jnp.arange(merged.shape[0], dtype=jnp.int32)
    indices = jnp.sum(chosen.astype(jnp.int32) * ladder[None, :], axis=1)
    filled = jnp.any(chosen, axis=1)
    return jnp.where(filled[:, None], merged[indices], jnp.zeros((), merged.dtype))


def body(
    patches,
    win_count,
    dest_perm,
    win_groups,
    norm_gain,
    qkv_weight,
    qkv_bias,
    proj_weight,
    proj_bias,
    merge_gain,
    owner,
):
    dev_count = lax.axis_size("dev")
    section_count = lax.axis_size("section")
    position = lax.axis_index("dev")
    windows = patches.reshape(SRC_WIN, WIN, D)
    counts = win_count[0]
    ladder = jnp.arange(dev_count, dtype=jnp.int32)
    before = jnp.sum(jnp.where(ladder[None, :] < ladder[:, None], counts[None, :], 0), axis=1)
    inverse = jnp.sum(
        ladder[:, None] * (dest_perm[0][:, None] == ladder[None, :]).astype(jnp.int32), axis=0
    )
    pair_slots = (SRC_WIN + dev_count - 1) // dev_count
    my_count = counts[position]
    begin_at = before[position]
    residue = jnp.mod(inverse - begin_at, dev_count)
    picked = jnp.arange(pair_slots, dtype=jnp.int32)[None, :] * dev_count + residue[:, None]
    usable = picked < my_count
    outgoing = jnp.where(
        usable[:, :, None, None],
        windows[jnp.minimum(picked, SRC_WIN - 1)],
        jnp.zeros((), windows.dtype),
    )
    outgoing = outgoing.reshape(dev_count * pair_slots * WIN, D)
    arrived = lax.all_to_all(outgoing, "dev", split_axis=0, concat_axis=0, tiled=True).reshape(
        dev_count, pair_slots, WIN, D
    )
    wanted = jnp.arange(DST_WIN, dtype=jnp.int32) * dev_count + inverse[position]
    source = jnp.sum((before[None, :] <= wanted[:, None]).astype(jnp.int32), axis=1) - 1
    within = wanted - before[source]
    balanced = arrived[source, within // dev_count]
    groups = win_groups[0][source, within]
    merged = encode(
        balanced, groups, norm_gain, qkv_weight, qkv_bias, proj_weight, proj_bias, merge_gain
    )
    merged_rows = merged.shape[0]
    capacity = 2 * merged_rows // section_count
    packed = pack(merged, owner[0, :, 0], section_count, capacity)
    delivered = lax.all_to_all(packed, "section", split_axis=0, concat_axis=0, tiled=True)
    return delivered.reshape(1, section_count * capacity, 4 * D)


def solution(mesh):
    return jax.shard_map(
        body,
        mesh=mesh,
        in_specs=(
            P("section", "dev", None),
            P("section", None),
            P("section", None),
            P("section", None, None),
            P(),
            P("dev", None),
            P(),
            P("dev", None),
            P(),
            P(),
            P("section", "dev", None),
        ),
        out_specs=P("section", "dev", None),
        check_vma=False,
    )
```

profile of v0, /device:TPU:1, one launch (start us, length us, event | category | flops | bytes accessed | tf_op | source)
XLA Modules:
  0.0 325.2 jit_solution(17619789578634482331)
XLA Ops:
  6.5 0.7 all-gather.3.cloned.1.call-update
  7.3 1.2 constant_dynamic-slice_fusion
  8.5 0.8 select_reduce_fusion.2
  9.3 0.6 dynamic_slice.9
  9.9 0.7 select_reduce_fusion.3
  10.6 0.7 fusion.20
  11.3 5.3 %gather_fusion = bf16[32,64,1280]{2,1,0:T(8,128)(2,1)} fusion(bf16[24,64,1280]{2,1,0:T(8,128)(2,1)} %bitcast.76, s32[1024]{0:T(1024)S(1)} %pad_clamp_fusion.2), kind=kCustom, calls=%fused_computation | custom fusion | bytes 10485888 | tf_op jit(solution)/shard_map/gather | solution.py:89
  16.6 1.2 fusion.16
  17.8 5.2 %broadcast_select_fusion = bf16[32,64,1280]{2,1,0:T(8,128)(2,1)} fusion(bf16[32,64,1280]{2,1,0:T(8,128)(2,1)} %gather_fusion, pred[32]{0:T(512)(128)(4,1)S(1)} %fusion.16), kind=kLoop, calls=%fused_computation.7 | loop fusion | flops 2621440 | bytes 10485792 | tf_op jit(solution)/shard_map/jit(_where)/select_n | solution.py:87
  23.0 12.8 %all-to-all-start = ((bf16[32,64,1280]{2,1,0:T(8,128)(2,1)}), bf16[32,64,1280]{2,1,0:T(8,128)(2,1)}, u32[]{:S(2)}, u32[]{:S(2)}) async-start(bf16[32,64,1280]{2,1,0:T(8,128)(2,1)} %broadcast_select_fusion), calls=%async_computation | async-start | bytes 10485760 | tf_op jit(solution)/shard_map/all_to_all | solution.py:93
  35.7 0.0 all-gather.5.cloned.1.call-start
  35.8 0.7 all-gather.5.cloned.1.call-update
  36.5 0.6 dynamic_slice.11
  37.1 0.6 multiply_add_fusion
  37.7 0.2 convert_reduce_fusion
  37.9 0.6 gather_fusion.1
  38.6 0.7 fusion.25
  39.3 0.6 gather_fusion.3
  39.9 0.1 fusion.29
  40.0 0.1 reshape.328
  40.1 0.1 fusion.12
  40.2 0.2 reduce_window_sum.11
  40.3 0.2 select_reduce_fusion.1
  40.5 0.1 fusion.11
  40.6 0.1 broadcast_in_dim.46
  40.7 0.1 select_reduce_fusion
  40.9 138.5 %all-to-all-done = bf16[32,64,1280]{2,1,0:T(8,128)(2,1)} async-done(((bf16[32,64,1280]{2,1,0:T(8,128)(2,1)}), bf16[32,64,1280]{2,1,0:T(8,128)(2,1)}, u32[]{:S(2)}, u32[]{:S(2)}) %all-to-all-start) | async-done | bytes 5242912 | tf_op jit(solution)/shard_map/all_to_all | solution.py:93
  179.4 3.2 gather_fusion.2
  182.6 0.3 multiply_reduce_fusion.1
  182.9 0.1 rsqrt.20
  183.0 0.4 fusion.4
  183.4 2.0 all-gather.3.cloned.1.call-done
  185.4 10.7 %add_convert_fusion = bf16[512,3840]{1,0:T(8,128)(2,1)} fusion(bf16[512,1280]{1,0:T(8,128)(2,1)S(1)} %fusion.4, bf16[1280,3840]{1,0:T(8,128)(2,1)} %all-gather.3.cloned.1.call-done, f32[3840]{0:T(1024)S(1)} %copy-done.5), kind=kOutput, calls=%fused_computation.6 | convolution fusion | flops 5037096960 | bytes 15088640 | tf_op jit(solution)/shard_map/dot_general | solution.py:19
  196.1 12.9 %reshape.324 = bf16[8,64,3,16,80]{4,3,2,1,0:T(8,128)(2,1)} reshape(bf16[512,3840]{1,0:T(8,128)(2,1)} %add_convert_fusion) | data formatting | bytes 7864320 | tf_op jit(solution)/shard_map/reshape | solution.py:27
  208.9 4.5 %fusion.30 = (bf16[8,64,1,16,80]{4,3,2,1,0:T(8,128)(2,1)S(1)}, bf16[8,64,1,16,80]{4,3,2,1,0:T(8,128)(2,1)S(1)}, bf16[8,64,1,16,80]{4,3,2,1,0:T(8,128)(2,1)S(1)}) fusion(bf16[8,64,3,16,80]{4,3,2,1,0:T(8,128)(2,1)} %reshape.324), kind=kLoop, calls=%fused_computation.86 | loop fusion | bytes 7864320 | tf_op jit(solution)/shard_map/slice | solution.py:38
  213.5 1.2 fusion.6
  214.7 2.3 fusion.31
  217.0 1.2 convert_bitcast_fusion
  218.2 1.4 copy.25
  219.6 3.3 %reshape.325 = bf16[512,1280]{1,0:T(8,128)(2,1)} reshape(bf16[8,64,16,80]{3,2,1,0:T(8,128)(2,1)S(1)} %copy.25) | data formatting | bytes 2621440 | tf_op jit(solution)/shard_map/reshape | solution.py:40
  222.9 47.1 %all-gather.5.cloned.1.call-done = bf16[1280,1280]{1,0:T(8,128)(2,1)} async-done(((bf16[40,1280]{1,0:T(8,128)(2,1)}), bf16[1280,1280]{1,0:T(8,128)(2,1)}) %all-gather.5.cloned.1.call-update) | async-done | bytes 3276816 | tf_op jit(solution)/shard_map/all_gather | solution.py:18
  270.0 4.4 %multiply_reduce_fusion = (f32[512]{0:T(512)S(1)}, f32[512,1280]{1,0:T(8,128)S(1)}) fusion(f32[1280]{0:T(1024)S(1)} %copy-done.6, bf16[512,1280]{1,0:T(8,128)(2,1)} %reshape.325, bf16[1280,1280]{1,0:T(8,128)(2,1)} %all-gather.5.cloned.1.call-done, bf16[512,1280]{1,0:T(8,128)(2,1)S(1)} %bitcast.73), kind=kOutput, calls=%fused_computation.18 | convolution fusion | flops 1680997888 | bytes 8526848 | tf_op jit(solution)/shard_map/dot_general | solution.py:19
  274.4 0.4 multiply_convert_fusion
  274.8 0.8 convert_element_type.62
  275.7 3.6 %gather_fusion.4 = bf16[256,5120]{1,0:T(8,128)(2,1)} fusion(bf16[128,5120]{1,0:T(8,128)(2,1)S(1)} %convert_element_type.62, s32[1024]{0:T(1024)S(1)} %pad_clamp_fusion), kind=kCustom, calls=%fused_computation.4 | custom fusion | bytes 5243904 | tf_op jit(solution)/shard_map/gather | solution.py:55
  279.2 2.0 broadcast_select_fusion.1
  281.2 35.6 %all_to_all.12 = bf16[8,32,5120]{2,1,0:T(8,128)(2,1)S(1)} all-to-all(bf16[8,32,5120]{2,1,0:T(8,128)(2,1)S(1)} %broadcast_select_fusion.1), channel_id=1, replica_groups=mesh['section'=8,'dev'=32] {'section'}, dimensions={0} | all-to-all | bytes 5242880 | tf_op jit(solution)/shard_map/all_to_all | solution.py:107
  316.9 1.5 copy.39
  (24 shorter events, 0.1 us)
Async XLA Ops:
  6.5 32.7 %copy-start = (s32[1,32,24]{1,2,0:T(8,128)S(1)}, s32[1,32,24]{1,2,0:T(8,128)}, u32[]{:S(2)}) copy-start(s32[1,32,24]{1,2,0:T(8,128)} %param.14) | copy-start | bytes 9220
  6.5 178.8 %all-gather.3.cloned.1.call-start = ((), (), s32[]{:S(2)}) async-start(), calls=%async_computation.2 | async-start | bytes 10137600 | tf_op jit(solution)/shard_map/all_gather | solution.py:18
  22.9 17.1 %copy-start.4 = (s32[1,128,1]{1,2,0:T(1,128)S(1)}, s32[1,128,1]{1,2,0:T(1,128)}, u32[]{:S(2)}) copy-start(s32[1,128,1]{1,2,0:T(1,128)} %param.21) | copy-start | bytes 1540
  23.0 156.4 %all-to-all-start = ((bf16[32,64,1280]{2,1,0:T(8,128)(2,1)}), bf16[32,64,1280]{2,1,0:T(8,128)(2,1)}, u32[]{:S(2)}, u32[]{:S(2)}) async-start(bf16[32,64,1280]{2,1,0:T(8,128)(2,1)} %broadcast_select_fusion), calls=%async_computation | async-start | bytes 10485760 | tf_op jit(solution)/shard_map/all_to_all | solution.py:93
  35.7 234.3 %all-gather.5.cloned.1.call-start = ((), (), s32[]{:S(2)}) async-start(), calls=%async_computation.3 | async-start | bytes 3379200 | tf_op jit(solution)/shard_map/all_gather | solution.py:18
  37.9 145.1 %copy-start.2 = (f32[1280]{0:T(1024)S(1)}, f32[1280]{0:T(1024)}, u32[]{:S(2)}) copy-start(f32[1280]{0:T(1024)} %param.15) | copy-start | bytes 15364
  182.6 2.8 copy-start.5
  219.6 50.4 %copy-start.6 = (f32[1280]{0:T(1024)S(1)}, f32[1280]{0:T(1024)}, u32[]{:S(2)}) copy-start(f32[1280]{0:T(1024)} %param.19) | copy-start | bytes 15364
  270.0 4.4 %copy-start.3 = (f32[1280]{0:T(1024)S(1)}, f32[1280]{0:T(1024)}, u32[]{:S(2)}) copy-start(f32[1280]{0:T(1024)} %param.20) | copy-start | bytes 15364
  316.9 1.5 copy-start.1
Sparse Core Ops, SparseCore 0:
  10.0 175.2 all-gather.2
  188.1 81.9 all-gather.4
where the time goes:
time: 326 us; the launch traced here: 325 us
  waiting for transfers between devices  189 us (58%)
  local copies, waits for them, and re-layouts  40.5 us (12%)
  blocking collectives  35.6 us (11%)
  matrix products  17.5 us (5%)
  other arithmetic  16.2 us (5%)
  between operations  13.6 us (4%)
  starting transfers between devices  12.8 us (4%)
    all_to_all x1, waiting for transfers between devices, body(): lax.all_to_all(outgoing, 'dev', split_axis=0, concat_axis=0, tiled=True)  138 us
    all_gather x2, waiting for transfers between devices, contract(): whole = lax.all_gather(shard, 'dev', axis=0, tiled=True)  49.1 us
    all_to_all x1, blocking collectives, body(): lax.all_to_all(packed, 'section', split_axis=0, concat_axis=0, tiled=True)  35.6 us
    dot_general x2, matrix products, contract(): return jnp.dot(inputs, whole, preferred_element_type=jnp.float32)  15 us
    reshape x1, local copies, waits for them, and re-layouts, encode(): triple = triple.reshape(count, WIN, 3, HEADS, D // HEADS)  12.9 us
    all_to_all x1, starting transfers between devices, body(): lax.all_to_all(outgoing, 'dev', split_axis=0, concat_axis=0, tiled=True)  12.8 us
  transfers between devices with their start and end apart: 3, of which 3 were waited for; matrix products, arithmetic and copies ran while one was open for 19% of the time, Pallas kernels for 0%

commit v1 on v0

--- a/solution.py
+++ b/solution.py
@@ -15,7 +15,9 @@
 
 
 def contract(inputs, shard):
-    whole = lax.all_gather(shard, "dev", axis=0, tiled=True)
+    o_now = jnp.stack([shard] * lax.axis_size("dev"), axis=0)
+    passed = lax.all_to_all(o_now, axis_name="dev", split_axis=0, concat_axis=0)
+    whole = jnp.concatenate(passed, axis=0)
     return jnp.dot(inputs, whole, preferred_element_type=jnp.float32)
 
 

time: 326 us -> 510 us (1.56)
  blocking collectives: 35.6 us -> 166 us
  waiting for transfers between devices: 189 us -> 247 us
  between operations: 13.6 us -> 0.25 us
  local copies, waits for them, and re-layouts: 40.5 us -> 46.8 us
  starting transfers between devices: 12.8 us -> 18.2 us
    all_to_all x0 -> x1, blocking collectives: none -> 130 us  [body(): lax.all_to_all(outgoing, 'dev', split_axis=0, concat_axis=0, tiled=True)]
    all_to_all x1 -> x2, waiting for transfers between devices: 138 us -> 247 us  [contract(): passed = lax.all_to_all(o_now, axis_name='dev', split_axis=0, concat_axis=0)]
    all_gather x2 -> x0, waiting for transfers between devices: 49.1 us -> none  [contract(): whole = lax.all_gather(shard, 'dev', axis=0, tiled=True)]
    another operation x0 -> x2, local copies, waits for them, and re-layouts: none -> 6.41 us  [contract(): o_now = jnp.stack([shard] * lax.axis_size('dev'), axis=0)]
    all_to_all x1 -> x2, starting transfers between devices: 12.8 us -> 18.2 us  [contract(): passed = lax.all_to_all(o_now, axis_name='dev', split_axis=0, concat_axis=0)]
  transfers between devices with their start and end apart: 3 -> 2, of which waited for: 3 -> 2; matrix products, arithmetic and copies ran while one was open for 19% -> 9% of each run, Pallas kernels for 0% -> 0%
where the time goes in v1:
time: 510 us; the launch traced here: 509 us
  waiting for transfers between devices  247 us (48%)
  blocking collectives  166 us (33%)
  local copies, waits for them, and re-layouts  46.8 us (9%)
  starting transfers between devices  18.2 us (4%)
  matrix products  17.5 us (3%)
  other arithmetic  14.1 us (3%)
    all_to_all x2, waiting for transfers between devices, contract(): passed = lax.all_to_all(o_now, axis_name='dev', split_axis=0, concat_axis=0)  247 us
    all_to_all x1, blocking collectives, body(): lax.all_to_all(outgoing, 'dev', split_axis=0, concat_axis=0, tiled=True)  130 us
    all_to_all x1, blocking collectives, body(): lax.all_to_all(packed, 'section', split_axis=0, concat_axis=0, tiled=True)  35.4 us
    all_to_all x2, starting transfers between devices, contract(): passed = lax.all_to_all(o_now, axis_name='dev', split_axis=0, concat_axis=0)  18.2 us
    dot_general x2, matrix products, contract(): return jnp.dot(inputs, whole, preferred_element_type=jnp.float32)  15.1 us
    reshape x1, local copies, waits for them, and re-layouts, encode(): triple = triple.reshape(count, WIN, 3, HEADS, D // HEADS)  12.9 us
  transfers between devices with their start and end apart: 2, of which 2 were waited for; matrix products, arithmetic and copies ran while one was open for 9% of the time, Pallas kernels for 0%

profile of v1, /device:TPU:1, one launch (start us, length us, event | category | flops | bytes accessed | tf_op | source)
XLA Modules:
  0.0 509.5 jit_solution(13662664592954651617)
XLA Ops:
  0.0 0.8 select_reduce_fusion.3
  0.8 0.8 select_reduce_fusion.2
  1.5 1.3 constant_dynamic-slice_fusion
  2.8 0.6 dynamic_slice.9
  3.4 0.7 fusion.18
  4.1 1.3 fusion.14
  5.5 5.3 %gather_fusion = bf16[32,64,1280]{2,1,0:T(8,128)(2,1)} fusion(bf16[24,64,1280]{2,1,0:T(8,128)(2,1)} %bitcast.75, s32[1024]{0:T(1024)S(1)} %pad_clamp_fusion.2), kind=kCustom, calls=%fused_computation | custom fusion | bytes 10485888 | tf_op jit(solution)/shard_map/gather | solution.py:91
  10.8 2.9 broadcast_select_fusion
  13.7 130.2 %all_to_all.22 = bf16[32,64,1280]{2,1,0:T(8,128)(2,1)} all-to-all(bf16[32,64,1280]{2,1,0:T(8,128)(2,1)S(1)} %broadcast_select_fusion), channel_id=1, replica_groups=mesh['section'=8,'dev'=32] {'dev'}, dimensions={0} | all-to-all | bytes 10485760 | tf_op jit(solution)/shard_map/all_to_all | solution.py:95
  143.9 4.4 stack.4
  148.3 7.1 %all-to-all-start.1 = ((bf16[32,40,3840]{2,1,0:T(8,128)(2,1)}), bf16[32,40,3840]{2,1,0:T(8,128)(2,1)}, u32[]{:S(2)}, u32[]{:S(2)}) async-start(bf16[32,40,3840]{2,1,0:T(8,128)(2,1)} %stack.4), calls=%async_computation.1 | async-start | bytes 19660800 | tf_op jit(solution)/shard_map/all_to_all | solution.py:19
  155.4 0.6 dynamic_slice.11
  156.0 0.6 multiply_add_fusion
  156.7 0.2 convert_reduce_fusion
  156.8 214.9 %all-to-all-done.1 = bf16[32,40,3840]{2,1,0:T(8,128)(2,1)} async-done(((bf16[32,40,3840]{2,1,0:T(8,128)(2,1)}), bf16[32,40,3840]{2,1,0:T(8,128)(2,1)}, u32[]{:S(2)}, u32[]{:S(2)}) %all-to-all-start.1) | async-done | bytes 9830432 | tf_op jit(solution)/shard_map/all_to_all | solution.py:19
  371.7 2.0 stack.5
  373.7 11.1 %all-to-all-start.2 = ((bf16[32,40,1280]{2,1,0:T(8,128)(2,1)}), bf16[32,40,1280]{2,1,0:T(8,128)(2,1)}, u32[]{:S(2)}, u32[]{:S(2)}) async-start(bf16[32,40,1280]{2,1,0:T(8,128)(2,1)} %stack.5), calls=%async_computation.2 | async-start | bytes 6553600 | tf_op jit(solution)/shard_map/all_to_all | solution.py:19
  384.9 0.0 copy-start.4
  384.9 0.6 gather_fusion.1
  385.6 0.7 fusion.23
  386.2 0.6 gather_fusion.3
  386.9 0.1 fusion.27
  387.0 0.1 reshape.381
  387.0 0.1 fusion.10
  387.1 0.2 reduce_window_sum.11
  387.3 0.2 select_reduce_fusion.1
  387.5 0.1 fusion.9
  387.6 0.1 broadcast_in_dim.46
  387.7 0.1 select_reduce_fusion
  387.9 3.1 gather_fusion.2
  391.0 0.3 multiply_reduce_fusion.1
  391.3 0.4 multiply_convert_fusion.1
  391.7 10.7 %add_convert_fusion = bf16[512,3840]{1,0:T(8,128)(2,1)} fusion(bf16[512,1280]{1,0:T(8,128)(2,1)S(1)} %bitcast.76, bf16[1280,3840]{1,0:T(8,128)(2,1)} %bitcast.17, f32[3840]{0:T(1024)S(1)} %copy-done.7), kind=kOutput, calls=%fused_computation.6 | convolution fusion | flops 5037096960 | bytes 15088640 | tf_op jit(solution)/shard_map/dot_general | solution.py:21
  402.4 12.9 %reshape.376 = bf16[8,64,3,16,80]{4,3,2,1,0:T(8,128)(2,1)} reshape(bf16[512,3840]{1,0:T(8,128)(2,1)} %add_convert_fusion) | data formatting | bytes 7864320 | tf_op jit(solution)/shard_map/reshape | solution.py:29
  415.3 4.5 fusion.28
  419.8 1.2 fusion.4
  421.1 2.3 fusion.29
  423.4 1.2 convert_bitcast_fusion
  424.6 1.4 copy.25
  426.0 3.3 reshape.377
  429.3 32.1 %all-to-all-done.2 = bf16[32,40,1280]{2,1,0:T(8,128)(2,1)} async-done(((bf16[32,40,1280]{2,1,0:T(8,128)(2,1)}), bf16[32,40,1280]{2,1,0:T(8,128)(2,1)}, u32[]{:S(2)}, u32[]{:S(2)}) %all-to-all-start.2) | async-done | bytes 3276832 | tf_op jit(solution)/shard_map/all_to_all | solution.py:19
  461.4 4.4 multiply_reduce_fusion
  465.8 0.4 multiply_convert_fusion
  466.2 0.8 convert_element_type.79
  467.0 3.6 gather_fusion.4
  470.6 2.0 broadcast_select_fusion.1
  472.5 35.4 %all_to_all.23 = bf16[8,32,5120]{2,1,0:T(8,128)(2,1)S(1)} all-to-all(bf16[8,32,5120]{2,1,0:T(8,128)(2,1)S(1)} %broadcast_select_fusion.1), channel_id=1, replica_groups=mesh['section'=8,'dev'=32] {'section'}, dimensions={0} | all-to-all | bytes 5242880 | tf_op jit(solution)/shard_map/all_to_all | solution.py:109
  508.0 1.5 copy.39
  (26 shorter events, 0.1 us)
Async XLA Ops:
  0.0 386.2 %copy-start = (s32[1,32,24]{1,2,0:T(8,128)S(1)}, s32[1,32,24]{1,2,0:T(8,128)}, u32[]{:S(2)}) copy-start(s32[1,32,24]{1,2,0:T(8,128)} %param.14) | copy-start | bytes 9220
  13.7 130.3 %copy-start.2 = (bf16[40,3840]{1,0:T(8,128)(2,1)S(1)}, bf16[40,3840]{1,0:T(8,128)(2,1)}, u32[]{:S(2)}) copy-start(bf16[40,3840]{1,0:T(8,128)(2,1)} %param.16) | copy-start | bytes 921604
  148.3 223.4 %copy-start.3 = (bf16[40,1280]{1,0:T(8,128)(2,1)S(1)}, bf16[40,1280]{1,0:T(8,128)(2,1)}, u32[]{:S(2)}) copy-start(bf16[40,1280]{1,0:T(8,128)(2,1)} %param.18) | copy-start | bytes 307204
  148.3 223.4 %all-to-all-start.1 = ((bf16[32,40,3840]{2,1,0:T(8,128)(2,1)}), bf16[32,40,3840]{2,1,0:T(8,128)(2,1)}, u32[]{:S(2)}, u32[]{:S(2)}) async-start(bf16[32,40,3840]{2,1,0:T(8,128)(2,1)} %stack.4), calls=%async_computation.1 | async-start | bytes 19660800 | tf_op jit(solution)/shard_map/all_to_all | solution.py:19
  373.7 13.3 %copy-start.6 = (s32[1,128,1]{1,2,0:T(1,128)S(1)}, s32[1,128,1]{1,2,0:T(1,128)}, u32[]{:S(2)}) copy-start(s32[1,128,1]{1,2,0:T(1,128)} %param.21) | copy-start | bytes 1540
  373.7 87.6 %all-to-all-start.2 = ((bf16[32,40,1280]{2,1,0:T(8,128)(2,1)}), bf16[32,40,1280]{2,1,0:T(8,128)(2,1)}, u32[]{:S(2)}, u32[]{:S(2)}) async-start(bf16[32,40,1280]{2,1,0:T(8,128)(2,1)} %stack.5), calls=%async_computation.2 | async-start | bytes 6553600 | tf_op jit(solution)/shard_map/all_to_all | solution.py:19
  384.9 6.4 %copy-start.4 = (f32[1280]{0:T(1024)S(1)}, f32[1280]{0:T(1024)}, u32[]{:S(2)}) copy-start(f32[1280]{0:T(1024)} %param.15) | copy-start | bytes 15364
  391.0 0.7 copy-start.7
  425.9 35.4 %copy-start.8 = (f32[1280]{0:T(1024)S(1)}, f32[1280]{0:T(1024)}, u32[]{:S(2)}) copy-start(f32[1280]{0:T(1024)} %param.19) | copy-start | bytes 15364
  461.4 4.4 copy-start.5
  508.0 1.5 copy-start.1
